TPU v7x, 32 devices: a whole 2x2x4 slice. The times are simulated.
32 devices in a mesh: dp: 8 (over y, x, core), tensor: 4 (over z).
Axes of the slice: x: 2, y: 2, z: 4, core: 2. Of those that a mesh axis runs over, the one named last changes fastest.
Arguments:
- tokens: bfloat16 [16384, 1536], P('dp'), may hold values from -6 to 6
- cotangent: bfloat16 [16384, 1536], P('dp'), may hold values from -6 to 6
- destination: int32 [16384], P('dp'), may hold values from 0 to 16383, as said below
- lengths: int32 [8, 4], P('dp'), may hold values from 1 to 1024, 2048 in all within a row
- norm_gain: float32 [1536], replicated, may hold values from 0.1 to 1.9
- inner_weight: float32 [1536, 2, 3072], P('dp', None, 'tensor'), may hold values from -0.15625 to 0.15625
- shared_weight: float32 [1536, 256], P('dp'), may hold values from -0.15625 to 0.15625
- step_weight: float32 [1536, 48], P('dp', 'tensor'), may hold values from -0.15625 to 0.15625
- filter_weight: float32 [4, 3072], P(None, 'tensor'), may hold values from -3 to 3
- filter_bias: float32 [3072], P('tensor'), may hold values from -3 to 3
- shared_filter: float32 [4, 256], replicated, may hold values from -3 to 3
- shared_filter_bias: float32 [256], replicated, may hold values from -3 to 3
- step_bias: float32 [48], P('tensor'), may hold values from -6 to -2
- decay_log: float32 [48], P('tensor'), may hold values from 0 to 2.77
- skip_gain: float32 [48], P('tensor'), may hold values from 0.5 to 1.5
- gate_gain: float32 [3072], P('tensor'), may hold values from 0.1 to 1.9
- out_weight: float32 [1536, 3072], P('dp', 'tensor'), may hold values from -0.109375 to 0.109375
Outputs:
- layer_out: bfloat16 [16384, 1536], P('dp')
- input_grad: bfloat16 [16384, 1536], P('dp')
- norm_gain_grad: float32 [1536], replicated
- inner_weight_grad: float32 [1536, 2, 3072], P('dp', None, 'tensor')
- shared_weight_grad: float32 [1536, 256], P('dp')
- step_weight_grad: float32 [1536, 48], P('dp', 'tensor')
- filter_weight_grad: float32 [4, 3072], P(None, 'tensor')
- filter_bias_grad: float32 [3072], P('tensor')
- shared_filter_grad: float32 [4, 256], replicated
- shared_filter_bias_grad: float32 [256], replicated
- step_bias_grad: float32 [48], P('tensor')
- decay_log_grad: float32 [48], P('tensor')
- skip_gain_grad: float32 [48], P('tensor')
- gate_gain_grad: float32 [3072], P('tensor')
- out_weight_grad: float32 [1536, 3072], P('dp', 'tensor')
Inputs may be any that keep to these rules, and one draw needn't show every extreme that they name: destination is a permutation. The tokens at given positions s * 2048 to (s + 1) * 2048 - 1 that go to work block w take exactly the work positions w * 2048 + s * 256 to w * 2048 + (s + 1) * 256 - 1. `lengths`: each row sums to 2048, and its longest sequence has exactly 1024 tokens.
All inputs are finite; a program needn't handle non-finite values.
Results may differ from a plain program's by a relative error of at most 0.012.
Values may be sent and summed in bfloat16 or wider, within the bound.
No kernel may reach another device: no remote copies, remote signals or barrier semaphores. Data moves between devices by JAX's collectives and lax.ppermute only.
A program may use at most 256 MiB of HBM per device.

v0:
```python
import jax
import jax.numpy as jnp
from jax import lax
from jax.sharding import PartitionSpec as P

INNER = 3072
SPAN = 256
EPSILON = 1e-05
PRECISE = lax.Precision.HIGHEST


def segments_of(lengths, row_count):
    seq_ends = jnp.cumsum(lengths)
    seq_starts = seq_ends - lengths
    places = jnp.arange(row_count, dtype=jnp.int32)
    segment = jnp.sum((places[:, None] >= seq_ends[None, :]).astype(jnp.int32), axis=1)
    belongs = segment[:, None] == jnp.arange(lengths.shape[0], dtype=jnp.int32)[None, :]
    position = places - jnp.sum(jnp.where(belongs, seq_starts[None, :], 0), axis=1)
    return (segment, position)


def causal_filter(signal, kernel, offset_bias, position):
    result = offset_bias + kernel[0] * signal
    for offset in range(1, kernel.shape[0]):
        shifted = jnp.pad(signal, ((offset, 0), (0, 0)))[: signal.shape[0]]
        allowed = (position >= offset).astype(signal.dtype)
        result = result + kernel[offset] * shifted * allowed[:, None]
    return result


def mixer(
    inputs,
    shared,
    step_raw,
    filter_weight,
    filter_bias,
    shared_filter,
    shared_filter_bias,
    step_bias,
    decay_log,
    skip_gain,
    segment,
    position,
):
    row_count = inputs.shape[0]
    heads_here = step_bias.shape[0]
    state_size = shared.shape[1] // 2
    values = jax.nn.silu(causal_filter(inputs, filter_weight, filter_bias, position)).reshape(
        row_count, heads_here, -1
    )
    factors = jax.nn.silu(causal_filter(shared, shared_filter, shared_filter_bias, position))
    writes = factors[:, :state_size]
    read_vectors = factors[:, state_size:]
    step_size = jax.nn.softplus(step_raw + step_bias)
    log_decay = -step_size * jnp.exp(decay_log)
    blocks = row_count // SPAN
    causal = jnp.arange(SPAN)[:, None] >= jnp.arange(SPAN)[None, :]

    def blocked(whole_array):
        return whole_array.reshape((blocks, SPAN) + whole_array.shape[1:])

    def span_step(state_carry, block_item):
        memory, last_segment = state_carry
        value_blk, write_blk, read_blk, size_blk, decay_blk, segment_blk = block_item
        cumulative = jnp.cumsum(decay_blk, axis=0).T
        inside = causal & (segment_blk[:, None] == segment_blk[None, :])
        spread = cumulative[:, :, None] - cumulative[:, None, :]
        decays = jnp.exp(jnp.where(inside[None], spread, -jnp.inf))
        scores = jnp.dot(read_blk, write_blk.T, precision=PRECISE)
        mixing = scores[None] * decays * size_blk.T[:, None, :]
        local_out = jnp.einsum("hts,shp->thp", mixing, value_blk, precision=PRECISE)
        carried = (segment_blk == last_segment).astype(value_blk.dtype)
        entering = jnp.exp(cumulative).T * carried[:, None]
        remote_out = (
            jnp.einsum("tn,hnp->thp", read_blk, memory, precision=PRECISE) * entering[:, :, None]
        )
        block_out = local_out + remote_out + skip_gain[None, :, None] * value_blk
        end_segment = segment_blk[-1]
        closing = (segment_blk == end_segment).astype(value_blk.dtype)
        weights = jnp.exp(cumulative[:, -1:] - cumulative) * size_blk.T * closing[None, :]
        added_state = jnp.einsum("sn,hs,shp->hnp", write_blk, weights, value_blk, precision=PRECISE)
        keeping = jnp.exp(cumulative[:, -1]) * (last_segment == end_segment).astype(value_blk.dtype)
        memory = memory * keeping[:, None, None] + added_state
        return ((memory, end_segment), block_out)

    initial = (jnp.zeros((heads_here, state_size, values.shape[2]), values.dtype), jnp.int32(-1))
    unused, outputs = lax.scan(
        jax.checkpoint(span_step),
        initial,
        (
            blocked(values),
            blocked(writes),
            blocked(read_vectors),
            blocked(step_size),
            blocked(log_decay),
            blocked(segment),
        ),
    )
    return outputs.reshape(row_count, -1)


def prenorm(hidden_in, norm_gain):
    scale = lax.rsqrt(jnp.mean(hidden_in * hidden_in, axis=1, keepdims=True) + EPSILON)
    return hidden_in * scale * norm_gain


def on_device(
    tokens,
    cotangent,
    destination,
    lengths,
    norm_gain,
    inner_weight,
    shared_weight,
    step_weight,
    filter_weight,
    filter_bias,
    shared_filter,
    shared_filter_bias,
    step_bias,
    decay_log,
    skip_gain,
    gate_gain,
    out_weight,
):
    row_count = tokens.shape[0]
    model_width = tokens.shape[1]
    group_rows = row_count // lax.axis_size("dp")
    my_index = lax.axis_index("dp")
    target_block = destination // row_count
    send_slot = (
        target_block * group_rows + (destination - target_block * row_count) - my_index * group_rows
    )
    send_order = (
        jnp.zeros((row_count,), jnp.int32).at[send_slot].set(jnp.arange(row_count, dtype=jnp.int32))
    )
    send_tokens = tokens[send_order]
    send_cot = cotangent[send_order]
    work_tokens, work_cot = (
        lax.all_to_all(send_tokens, "dp", split_axis=0, concat_axis=0, tiled=True),
        lax.all_to_all(send_cot, "dp", split_axis=0, concat_axis=0, tiled=True),
    )
    inner_full, shared_full, step_full, out_full = (
        lax.all_gather(inner_weight.astype(jnp.bfloat16), "dp", axis=0, tiled=True),
        lax.all_gather(shared_weight.astype(jnp.bfloat16), "dp", axis=0, tiled=True),
        lax.all_gather(step_weight.astype(jnp.bfloat16), "dp", axis=0, tiled=True),
        lax.all_gather(out_weight.astype(jnp.bfloat16), "dp", axis=0, tiled=True),
    )
    col_share = model_width // lax.axis_size("tensor")
    column = lax.axis_index("tensor") * col_share
    hidden_in = work_tokens.astype(jnp.float32)
    segment, position = segments_of(lengths[0], row_count)
    normed, pull_norm = jax.vjp(prenorm, hidden_in, norm_gain)
    normed_low = normed.astype(jnp.bfloat16)
    inner_flat = inner_full.reshape(inner_full.shape[0], -1)
    both = jnp.dot(normed_low, inner_flat, preferred_element_type=jnp.float32)
    half_width = both.shape[1] // 2
    gate_in = both[:, :half_width]
    inputs = both[:, half_width:]
    shared = jnp.dot(normed_low, shared_full, preferred_element_type=jnp.float32)
    step_raw = jnp.dot(normed_low, step_full, preferred_element_type=jnp.float32)

    def local_mixer(
        inputs,
        shared,
        step_raw,
        filter_weight,
        filter_bias,
        shared_filter,
        shared_filter_bias,
        step_bias,
        decay_log,
        skip_gain,
    ):
        return mixer(
            inputs,
            shared,
            step_raw,
            filter_weight,
            filter_bias,
            shared_filter,
            shared_filter_bias,
            step_bias,
            decay_log,
            skip_gain,
            segment,
            position,
        )

    mixed_in, pull_mixer = jax.vjp(
        local_mixer,
        inputs,
        shared,
        step_raw,
        filter_weight,
        filter_bias,
        shared_filter,
        shared_filter_bias,
        step_bias,
        decay_log,
        skip_gain,
    )
    gate_sig = jax.nn.sigmoid(gate_in)
    gate_act = gate_in * gate_sig
    gated = mixed_in * gate_act
    square_sum = lax.psum(jnp.sum(gated * gated, axis=1), "tensor")
    gate_scale = lax.rsqrt(square_sum / INNER + EPSILON)[:, None]
    gate_normed = (gated * gate_scale * gate_gain).astype(jnp.bfloat16)
    partial_out = jnp.einsum("ti,di->td", gate_normed, out_full, preferred_element_type=jnp.float32)
    branch = lax.psum(partial_out, "tensor")
    layer_work = (hidden_in + branch).astype(jnp.bfloat16)
    part_out = lax.dynamic_slice_in_dim(layer_work, column, col_share, 1)
    out_grad = jnp.einsum("td,ti->di", work_cot, gate_normed, preferred_element_type=jnp.float32)
    normed_grad = jnp.einsum("td,di->ti", work_cot, out_full, preferred_element_type=jnp.float32)
    gate_gain_grad = jnp.sum(normed_grad * gated * gate_scale, axis=0)
    scaled_grad = normed_grad * gate_gain
    cross_sum = lax.psum(jnp.sum(scaled_grad * gated, axis=1), "tensor")
    gated_grad = gate_scale * scaled_grad - gated * gate_scale**3 * (cross_sum / INNER)[:, None]
    mixed_grad = gated_grad * gate_act
    gate_in_grad = gated_grad * mixed_in * gate_sig * (1.0 + gate_in * (1.0 - gate_sig))
    (
        inputs_grad,
        shared_part,
        step_raw_grad,
        filter_weight_grad,
        filter_bias_grad,
        shared_filter_part,
        shared_bias_part,
        step_bias_grad,
        decay_log_grad,
        skip_gain_grad,
    ) = pull_mixer(mixed_grad)
    shared_grad, shared_filter_grad, shared_filter_bias_grad = lax.psum(
        (shared_part, shared_filter_part, shared_bias_part), "tensor"
    )
    both_low = jnp.concatenate([gate_in_grad, inputs_grad], axis=1).astype(jnp.bfloat16)
    shared_low = shared_grad.astype(jnp.bfloat16)
    step_low = step_raw_grad.astype(jnp.bfloat16)
    input_part = jnp.einsum("tk,dk->td", both_low, inner_flat, preferred_element_type=jnp.float32)
    input_part = input_part + jnp.einsum(
        "tk,dk->td", step_low, step_full, preferred_element_type=jnp.float32
    )
    normed_back = lax.psum(input_part, "tensor")
    normed_back = normed_back + jnp.einsum(
        "tk,dk->td", shared_low, shared_full, preferred_element_type=jnp.float32
    )
    input_norm_grad, norm_gain_grad = pull_norm(normed_back)
    input_work = (input_norm_grad + work_cot.astype(jnp.float32)).astype(jnp.bfloat16)
    part_grad = lax.dynamic_slice_in_dim(input_work, column, col_share, 1)
    inner_grad = jnp.einsum(
        "td,tk->dk", normed_low, both_low, preferred_element_type=jnp.float32
    ).reshape(inner_full.shape)
    shared_weight_grad = jnp.einsum(
        "td,tk->dk", normed_low, shared_low, preferred_element_type=jnp.float32
    )
    step_weight_grad = jnp.einsum(
        "td,tk->dk", normed_low, step_low, preferred_element_type=jnp.float32
    )
    inner_grad, shared_weight_grad, step_weight_grad, out_grad = (
        lax.psum_scatter(inner_grad, "dp", scatter_dimension=0, tiled=True),
        lax.psum_scatter(shared_weight_grad, "dp", scatter_dimension=0, tiled=True),
        lax.psum_scatter(step_weight_grad, "dp", scatter_dimension=0, tiled=True),
        lax.psum_scatter(out_grad, "dp", scatter_dimension=0, tiled=True),
    )
    (
        norm_gain_grad,
        filter_weight_grad,
        filter_bias_grad,
        shared_filter_grad,
        shared_filter_bias_grad,
        step_bias_grad,
        decay_log_grad,
        skip_gain_grad,
        gate_gain_grad,
    ) = lax.psum(
        (
            norm_gain_grad,
            filter_weight_grad,
            filter_bias_grad,
            shared_filter_grad,
            shared_filter_bias_grad,
            step_bias_grad,
            decay_log_grad,
            skip_gain_grad,
            gate_gain_grad,
        ),
        "dp",
    )
    part_out, part_grad = (
        lax.all_to_all(part_out, "dp", split_axis=0, concat_axis=0, tiled=True),
        lax.all_to_all(part_grad, "dp", split_axis=0, concat_axis=0, tiled=True),
    )
    back_out, back_grad = (
        lax.all_gather(part_out, "tensor", axis=1, tiled=True),
        lax.all_gather(part_grad, "tensor", axis=1, tiled=True),
    )
    layer_out = back_out[send_slot]
    input_grad = back_grad[send_slot]
    return (
        layer_out,
        input_grad,
        norm_gain_grad,
        inner_grad,
        shared_weight_grad,
        step_weight_grad,
        filter_weight_grad,
        filter_bias_grad,
        shared_filter_grad,
        shared_filter_bias_grad,
        step_bias_grad,
        decay_log_grad,
        skip_gain_grad,
        gate_gain_grad,
        out_grad,
    )


def solution(mesh):
    in_specs = (
        P("dp", None),
        P("dp", None),
        P("dp"),
        P("dp", None),
        P(),
        P("dp", None, "tensor"),
        P("dp", None),
        P("dp", "tensor"),
        P(None, "tensor"),
        P("tensor"),
        P(),
        P(),
        P("tensor"),
        P("tensor"),
        P("tensor"),
        P("tensor"),
        P("dp", "tensor"),
    )
    out_specs = (
        P("dp", None),
        P("dp", None),
        P(),
        P("dp", None, "tensor"),
        P("dp", None),
        P("dp", "tensor"),
        P(None, "tensor"),
        P("tensor"),
        P(),
        P(),
        P("tensor"),
        P("tensor"),
        P("tensor"),
        P("tensor"),
        P("dp", "tensor"),
    )
    return jax.shard_map(
        on_device, mesh=mesh, in_specs=in_specs, out_specs=out_specs, check_vma=False
    )
```

profile of v0, /device:TPU:0, one launch (start us, length us, event | category | flops | bytes accessed | tf_op | source)
XLA Modules:
  0.0 2527.5 jit_solution(8638867920375196014)
XLA Ops:
  19.1 17.3 gather_fusion
  42.7 88.8 %all-gather = bf16[8,192,12]{1,2,0:T(8,128)(2,1)S(1)} all-gather(bf16[1,192,12]{1,2,0:T(8,128)(2,1)S(1)} %convert_bitcast_fusion), channel_id=1, replica_groups=mesh['dp'=8,'tensor'=4] {'dp'}, dimensions={0}, use_global_device_ids=true | all-gather | bytes 41472 | tf_op jit(solution)/shard_map/all_gather | solution.py:146
  131.8 16.9 gather_fusion.2
  240.2 294.4 %while.47 = (s32[]{:T(128)}, f32[12,128,64]{1,2,0:T(8,128)S(1)}, s32[]{:T(128)}, f32[8,256,12,64]{1,0,3,2:T(8,128)}, f32[8,12,128,64]{2,3,1,0:T(8,128)}, /*index...) while((s32[]{:T(128)}, f32[12,128,64]{1,2,0:T(8,128)S(1)}, ...), condition=%wide.region_8.9_spmd.clone, body=%wide.region_5.8_spmd.clone.sunk | while | flops 1313649664 | bytes 11765497 | solution.py:87
  254.0 18.5 dynamic_update_slice.85
  290.8 18.5 dynamic_update_slice.85
  327.6 18.5 dynamic_update_slice.85
  364.4 18.5 dynamic_update_slice.85
  401.2 18.5 dynamic_update_slice.85
  438.0 18.5 dynamic_update_slice.85
  474.8 18.5 dynamic_update_slice.85
  511.6 18.5 dynamic_update_slice.85
  624.5 466.0 %while.48 = (s32[]{:T(128)}, f32[12]{0:T(128)}, f32[12,128,64]{1,2,0:T(8,128)S(1)}, f32[8,256,12,64]{1,0,3,2:T(8,128)}, f32[8,256,128]{2,1,0:T(8,128)}, /*index=...) while((s32[]{:T(128)}, f32[12]{0:T(128)}, ...), condition=%wide.region_27.28_spmd.clone, body=%wide.region_14.27_spmd.clone.sunk | while | flops 3037355008 | bytes 28656244 | solution.py:87
  657.0 18.5 dynamic_update_slice.89
  715.2 18.5 dynamic_update_slice.89
  773.4 18.5 dynamic_update_slice.89
  831.5 18.5 dynamic_update_slice.89
  889.7 18.5 dynamic_update_slice.89
  947.8 18.5 dynamic_update_slice.89
  1006.0 18.5 dynamic_update_slice.89
  1064.2 18.5 dynamic_update_slice.89
  1219.2 147.4 %all-reduce.31 = (bf16[2048,256]{1,0:T(8,128)(2,1)}, f32[4,256]{1,0:T(4,128)S(1)}, f32[256]{0:T(256)S(1)}) all-reduce(f32[2048,256]{1,0:T(8,128)S(1)} %fusion.111, f32[4,256]{1,0:T(4,128)S(1)} %pad_add_fusion.1, f32[256]{0:T(256)S(1)} %get-tuple-element.895), channel_id=1, replica_groups=mesh['dp'=8,'tensor'=4] {'tensor'}, use_global_device_ids=true, to_apply=%region_29.30 | all-reduce | flops 525568 | bytes 3155968 | tf_op jit(solution)/shard_map/psum | solution.py:233
  1366.6 702.3 %all-reduce.30.cloned.1.call-done = (f32[2048,1536]{1,0:T(8,128)}, f32[2048,1536]{1,0:T(8,128)}) async-done(((f32[2048,1536]{1,0:T(8,128)}, f32[2048,1536]{1,0:T(8,128)}), (f32[2048,1536]{1,0:T(8,128)}, f32[2048,1536]{1,0:T(8,128)})) %all-reduce.30.cloned.1.call-update) | async-done | bytes 25165840 | tf_op jit(solution)/shard_map/psum | solution.py:210
  2082.1 26.8 %all_to_all.45 = bf16[8,256,384]{2,1,0:T(8,128)(2,1)} all-to-all(bf16[8,256,384]{2,1,0:T(8,128)(2,1)S(1)} %bitcast.451), channel_id=1, replica_groups=mesh['dp'=8,'tensor'=4] {'dp'}, dimensions={0} | all-to-all | bytes 3145728 | tf_op jit(solution)/shard_map/all_to_all | solution.py:291
  2109.0 24.1 all_to_all.46
  2152.5 38.1 %reduce-scatter.7.cloned.1.call-done = f32[192,2,768]{2,0,1:T(8,128)} async-done(((f32[1536,2,768]{2,0,1:T(8,128)}), f32[192,2,768]{2,0,1:T(8,128)}) %reduce-scatter.7.cloned.1.call-update) | async-done | bytes 1179664 | tf_op jit(solution)/shard_map/reduce_scatter | solution.py:260
  2193.8 25.0 all-reduce.24
  2218.8 88.6 %all-gather.12.cloned.1.call-done = bf16[2048,1536]{1,0:T(8,128)(2,1)} async-done(((bf16[2048,384]{1,0:T(8,128)(2,1)}), bf16[2048,1536]{1,0:T(8,128)(2,1)}) %all-gather.12.cloned.1.call-update) | async-done | bytes 6291472 | tf_op jit(solution)/shard_map/all_gather | solution.py:295
  2307.4 16.8 gather_fusion.3
  2324.2 98.3 %all-gather.10.cloned.1.call-done = bf16[2048,1536]{1,0:T(8,128)(2,1)} async-done(((bf16[2048,384]{1,0:T(8,128)(2,1)}), bf16[2048,1536]{1,0:T(8,128)(2,1)}) %all-gather.10.cloned.1.call-update) | async-done | bytes 6291472 | tf_op jit(solution)/shard_map/all_gather | solution.py:294
  2439.3 23.6 reduce-scatter.9.cloned.1.call-done
  2462.9 57.8 %reduce-scatter.11.cloned.1.call-done = f32[192,768]{1,0:T(8,128)} async-done(((f32[1536,768]{1,0:T(8,128)}), f32[192,768]{1,0:T(8,128)}) %reduce-scatter.11.cloned.1.call-update) | async-done | bytes 589840 | tf_op jit(solution)/shard_map/reduce_scatter | solution.py:263
  (1035 shorter events, 820.6 us)
Async XLA Ops:
  7.2 182.1 %all-gather.6.cloned.1.call-start = ((), (), s32[]{:S(2)}) async-start(), calls=%async_computation.8 | async-start | bytes 5308416 | tf_op jit(solution)/shard_map/all_gather | solution.py:144
  36.4 95.1 %copy-start.73 = (f32[12]{0:T(128)S(1)}, f32[12]{0:T(128)}, u32[]{:S(2)}) copy-start(f32[12]{0:T(128)} %param.34) | copy-start | bytes 148
  36.4 122.0 %all-to-all-start = ((bf16[8,256,1536]{2,1,0:T(8,128)(2,1)}), bf16[8,256,1536]{2,1,0:T(8,128)(2,1)}, u32[]{:S(2)}, u32[]{:S(2)}) async-start(bf16[8,256,1536]{2,1,0:T(8,128)(2,1)} %bitcast.442), calls=%async_computation | async-start | bytes 12582912 | tf_op jit(solution)/shard_map/all_to_all | solution.py:140
  41.6 527.2 %all-gather.8.cloned.1.call-start = ((), (), s32[]{:S(2)}) async-start(), calls=%async_computation.9 | async-start | bytes 2654208 | tf_op jit(solution)/shard_map/all_gather | solution.py:147
  131.6 46.8 %copy-start.15 = (bf16[1536,12]{0,1:T(8,128)(2,1)}, bf16[1536,12]{0,1:T(8,128)(2,1)S(1)}, u32[]{:S(2)}) copy-start(bf16[1536,12]{0,1:T(8,128)(2,1)S(1)} %reshape.579) | copy-start | bytes 110596
  131.6 46.8 %copy-start.60 = (f32[12]{0:T(128)}, f32[12]{0:T(128)S(1)}, u32[]{:S(2)}) copy-start(f32[12]{0:T(128)S(1)} %exp.96) | copy-start | bytes 148
  148.8 62.9 %copy-start.37 = (f32[768]{0:T(1024)}, f32[768]{0:T(1024)S(1)}, u32[]{:S(2)}) copy-start(f32[768]{0:T(1024)S(1)} %get-tuple-element.897) | copy-start | bytes 9220
  148.8 62.8 %copy-start.39 = (f32[768]{0:T(1024)}, f32[768]{0:T(1024)S(1)}, u32[]{:S(2)}) copy-start(f32[768]{0:T(1024)S(1)} %get-tuple-element.898) | copy-start | bytes 9220
  148.8 62.8 %copy-start.41 = (f32[768]{0:T(1024)}, f32[768]{0:T(1024)S(1)}, u32[]{:S(2)}) copy-start(f32[768]{0:T(1024)S(1)} %get-tuple-element.899) | copy-start | bytes 9220
  148.8 62.8 %copy-start.43 = (f32[768]{0:T(1024)}, f32[768]{0:T(1024)S(1)}, u32[]{:S(2)}) copy-start(f32[768]{0:T(1024)S(1)} %get-tuple-element.896) | copy-start | bytes 9220
  158.4 53.3 %copy-start.17 = (f32[2048]{0:T(1024)}, f32[2048]{0:T(1024)S(1)}, u32[]{:S(2)}) copy-start(f32[2048]{0:T(1024)S(1)} %get-tuple-element.1029) | copy-start | bytes 24580
  158.4 53.3 %copy-start.19 = (f32[2048]{0:T(1024)}, f32[2048]{0:T(1024)S(1)}, u32[]{:S(2)}) copy-start(f32[2048]{0:T(1024)S(1)} %get-tuple-element.1030) | copy-start | bytes 24580
  158.4 53.3 %copy-start.21 = (f32[2048]{0:T(1024)}, f32[2048]{0:T(1024)S(1)}, u32[]{:S(2)}) copy-start(f32[2048]{0:T(1024)S(1)} %get-tuple-element.1031) | copy-start | bytes 24580
  158.4 410.3 %all-to-all-start.2 = ((bf16[8,256,1536]{2,1,0:T(8,128)(2,1)}), bf16[8,256,1536]{2,1,0:T(8,128)(2,1)}, u32[]{:S(2)}, u32[]{:S(2)}) async-start(bf16[8,256,1536]{2,1,0:T(8,128)(2,1)} %bitcast.441), calls=%async_computation.2 | async-start | bytes 12582912 | tf_op jit(solution)/shard_map/all_to_all | solution.py:141
  163.2 1905.6 %all-reduce.30.cloned.1.call-start = ((), (), s32[]{:S(2)}) async-start(), calls=%async_computation.16 | async-start | bytes 50331648 | tf_op jit(solution)/shard_map/psum | solution.py:210
  708.9 32.2 %copy-start.36 = (s32[8,256]{1,0:T(8,128)S(1)}, s32[8,256]{1,0:T(8,128)}, u32[]{:S(2)}) copy-start(s32[8,256]{1,0:T(8,128)} %copy-done.35) | copy-start | bytes 24580 | tf_op jit(solution)/shard_map/transpose(jvp())/while
  999.7 32.2 %copy-start.36 = (s32[8,256]{1,0:T(8,128)S(1)}, s32[8,256]{1,0:T(8,128)}, u32[]{:S(2)}) copy-start(s32[8,256]{1,0:T(8,128)} %copy-done.35) | copy-start | bytes 24580 | tf_op jit(solution)/shard_map/transpose(jvp())/while
  1057.9 32.2 %copy-start.36 = (s32[8,256]{1,0:T(8,128)S(1)}, s32[8,256]{1,0:T(8,128)}, u32[]{:S(2)}) copy-start(s32[8,256]{1,0:T(8,128)} %copy-done.35) | copy-start | bytes 24580 | tf_op jit(solution)/shard_map/transpose(jvp())/while
  1126.3 33.3 %slice-start = ((s8[6291456]{0:T(1024)(128)(4,1)}), s8[4194304]{0:T(1024)(128)(4,1)S(1)}, s32[]{:S(2)}) async-start(s8[6291456]{0:T(1024)(128)(4,1)} %bitcast.432), calls=%async_computation.17 | async-start | bytes 8388608
  1167.9 983.0 %reduce-scatter.13.cloned.1.call-start = ((), (), s32[]{:S(2)}) async-start(), calls=%async_computation.15 | async-start | bytes 884736
  1189.7 1000.9 %reduce-scatter.7.cloned.1.call-start = ((), (), s32[]{:S(2)}) async-start(), calls=%async_computation.12 | async-start | bytes 10616832 | tf_op jit(solution)/shard_map/reduce_scatter | solution.py:260
  1205.4 1102.0 %all-gather.12.cloned.1.call-start = ((), (), s32[]{:S(2)}) async-start(), calls=%async_computation.11 | async-start | bytes 7864320 | tf_op jit(solution)/shard_map/all_gather | solution.py:295
  1218.5 850.4 %copy-start.11 = (bf16[1536,256]{1,0:T(8,128)(2,1)S(1)}, bf16[1536,256]{1,0:T(8,128)(2,1)}, u32[]{:S(2)}) copy-start(bf16[1536,256]{1,0:T(8,128)(2,1)} %copy-done.10) | copy-start | bytes 2359300
  1218.5 850.4 %copy-start.29 = (f32[2048]{0:T(1024)S(1)}, f32[2048]{0:T(1024)}, u32[]{:S(2)}) copy-start(f32[2048]{0:T(1024)} %copy-done.28) | copy-start | bytes 24580
  1218.5 850.4 %copy-start.31 = (f32[1536]{0:T(1024)S(1)}, f32[1536]{0:T(1024)}, u32[]{:S(2)}) copy-start(f32[1536]{0:T(1024)} %param.25) | copy-start | bytes 18436
  2082.0 51.1 %copy-start.12 = (bf16[2048,256]{1,0:T(8,128)(2,1)S(1)}, bf16[2048,256]{1,0:T(8,128)(2,1)}, u32[]{:S(2)}) copy-start(bf16[2048,256]{1,0:T(8,128)(2,1)} %get-tuple-element.971) | copy-start | bytes 3145732
  2108.9 313.6 %all-gather.10.cloned.1.call-start = ((), (), s32[]{:S(2)}) async-start(), calls=%async_computation.10 | async-start | bytes 7864320 | tf_op jit(solution)/shard_map/all_gather | solution.py:294
  2133.1 329.8 %reduce-scatter.9.cloned.1.call-start = ((), (), s32[]{:S(2)}) async-start(), calls=%async_computation.13 | async-start | bytes 1769472 | tf_op jit(solution)/shard_map/reduce_scatter | solution.py:261
  2139.0 381.7 %reduce-scatter.11.cloned.1.call-start = ((), (), s32[]{:S(2)}) async-start(), calls=%async_computation.14 | async-start | bytes 5308416 | tf_op jit(solution)/shard_map/reduce_scatter | solution.py:263
  2150.7 43.0 %copy-start.49 = (f32[12]{0:T(128)S(1)}, f32[12]{0:T(128)}, u32[]{:S(2)}) copy-start(f32[12]{0:T(128)} %get-tuple-element.530) | copy-start | bytes 148
  2150.7 43.0 %copy-start.65 = (f32[768]{0:T(1024)S(1)}, f32[768]{0:T(1024)}, u32[]{:S(2)}) copy-start(f32[768]{0:T(1024)} %get-tuple-element.882) | copy-start | bytes 9220
  2150.7 156.6 %copy-start.34 = (s32[2048]{0:T(1024)S(1)}, s32[2048]{0:T(1024)}, u32[]{:S(2)}) copy-start(s32[2048]{0:T(1024)} %get-tuple-element.987) | copy-start | bytes 24580
  (105 other events, 1154.9 us)
Sparse Core Ops, SparseCore 0:
  10.4 46.6 all-gather.5
  59.0 70.6 all-gather.7
  1168.0 900.7 all-reduce.29
  2072.4 38.3 reduce-scatter.12
  2114.2 76.3 reduce-scatter.6
  2192.0 115.3 all-gather.11
  2308.9 113.5 all-gather.9
  2426.3 36.5 reduce-scatter.8
  2466.9 53.7 reduce-scatter.10
where the time goes:
time: 2550 us; the launch traced here: 2530 us
  waiting for transfers between devices  1010 us (40%)
  local copies, waits for them, and re-layouts  624 us (24%)
  blocking collectives  342 us (13%)
  matrix products  315 us (12%)
  other arithmetic  188 us (7%)
    psum x1, waiting for transfers between devices, on_device(): branch = lax.psum(partial_out, 'tensor')  702 us
    dynamic_update_slice x72, local copies, waits for them, and re-layouts, mixer(): lax.scan(jax.checkpoint(span_step), initial, (blocked(values), blocked(wr...  344 us
    psum x1, blocking collectives, on_device(): lax.psum((shared_part, shared_filter_part, shared_bias_part), 'tensor')  147 us
    dot_general x24, matrix products, span_step(): local_out = jnp.einsum('hts,shp->thp', mixing, value_blk, precision=PRECISE)  101 us
    all_gather x1, waiting for transfers between devices, on_device(): lax.all_gather(part_out, 'tensor', axis=1, tiled=True)  98.3 us
    all_gather x1, blocking collectives, on_device(): lax.all_gather(step_weight.astype(jnp.bfloat16), 'dp', axis=0, tiled=True)  88.8 us
    all_gather x1, waiting for transfers between devices, on_device(): lax.all_gather(part_grad, 'tensor', axis=1, tiled=True)  88.6 us
    reduce_scatter x1, waiting for transfers between devices, on_device(): lax.psum_scatter(out_grad, 'dp', scatter_dimension=0, tiled=True)  57.8 us
  transfers between devices with their start and end apart: 11, of which 6 were waited for; matrix products, arithmetic and copies ran while one was open for 21% of the time, Pallas kernels for 0%

commit v1 on v0

--- a/solution.py
+++ b/solution.py
@@ -207,7 +207,9 @@
     gate_scale = lax.rsqrt(square_sum / INNER + EPSILON)[:, None]
     gate_normed = (gated * gate_scale * gate_gain).astype(jnp.bfloat16)
     partial_out = jnp.einsum("ti,di->td", gate_normed, out_full, preferred_element_type=jnp.float32)
-    branch = lax.psum(partial_out, "tensor")
+    branch = partial_out
+    for hop in (1, 2):
+        branch = branch + lax.ppermute(branch, "tensor", [(dev, dev ^ hop) for dev in range(4)])
     layer_work = (hidden_in + branch).astype(jnp.bfloat16)
     part_out = lax.dynamic_slice_in_dim(layer_work, column, col_share, 1)
     out_grad = jnp.einsum("td,ti->di", work_cot, gate_normed, preferred_element_type=jnp.float32)

time: 2550 us -> 2820 us (1.11)
  blocking collectives: 342 us -> 804 us
  waiting for transfers between devices: 1010 us -> 815 us
    psum x1, waiting for transfers between devices: 702 us -> 0.01 us  [on_device(): normed_back = lax.psum(input_part, 'tensor')]
    ppermute x0 -> x2, waiting for transfers between devices: none -> 593 us  [on_device(): lax.ppermute(branch, 'tensor', [(dev, dev ^ hop) for dev in range(4)])]
    psum x1, blocking collectives: 147 us -> 611 us  [on_device(): lax.psum((shared_part, shared_filter_part, shared_bias_part), 'tensor')]
    all_gather x1, waiting for transfers between devices: 88.6 us -> 42.4 us  [on_device(): lax.all_gather(part_grad, 'tensor', axis=1, tiled=True)]
    reduce_scatter x1, waiting for transfers between devices: 38.1 us -> 0.01 us  [on_device(): lax.psum_scatter(inner_grad, 'dp', scatter_dimension=0, tiled=True)]
  transfers between devices with their start and end apart: 11 -> 13, of which waited for: 6 -> 5; matrix products, arithmetic and copies ran while one was open for 21% -> 20% of each run, Pallas kernels for 0% -> 0%
where the time goes in v1:
time: 2820 us; the launch traced here: 2800 us
  waiting for transfers between devices  815 us (29%)
  blocking collectives  804 us (29%)
  local copies, waits for them, and re-layouts  624 us (22%)
  matrix products  310 us (11%)
  other arithmetic  198 us (7%)
    psum x1, blocking collectives, on_device(): lax.psum((shared_part, shared_filter_part, shared_bias_part), 'tensor')  611 us
    ppermute x2, waiting for transfers between devices, on_device(): lax.ppermute(branch, 'tensor', [(dev, dev ^ hop) for dev in range(4)])  593 us
    dynamic_update_slice x72, local copies, waits for them, and re-layouts, mixer(): lax.scan(jax.checkpoint(span_step), initial, (blocked(values), blocked(wr...  345 us
    dot_general x24, matrix products, span_step(): local_out = jnp.einsum('hts,shp->thp', mixing, value_blk, precision=PRECISE)  101 us
    all_gather x1, waiting for transfers between devices, on_device(): lax.all_gather(part_out, 'tensor', axis=1, tiled=True)  98.3 us
    all_gather x1, blocking collectives, on_device(): lax.all_gather(step_weight.astype(jnp.bfloat16), 'dp', axis=0, tiled=True)  88.7 us
    reduce_scatter x1, waiting for transfers between devices, on_device(): lax.psum_scatter(out_grad, 'dp', scatter_dimension=0, tiled=True)  57.8 us
  transfers between devices with their start and end apart: 13, of which 5 were waited for; matrix products, arithmetic and copies ran while one was open for 20% of the time, Pallas kernels for 0%

profile of v1, /device:TPU:0, one launch (start us, length us, event | category | flops | bytes accessed | tf_op | source)
XLA Modules:
  0.0 2803.3 jit_solution(15248362805198247531)
XLA Ops:
  19.1 17.3 gather_fusion
  42.7 88.7 %all-gather = bf16[8,192,12]{1,2,0:T(8,128)(2,1)S(1)} all-gather(bf16[1,192,12]{1,2,0:T(8,128)(2,1)S(1)} %convert_bitcast_fusion), channel_id=1, replica_groups=mesh['dp'=8,'tensor'=4] {'dp'}, dimensions={0}, use_global_device_ids=true | all-gather | bytes 41472 | tf_op jit(solution)/shard_map/all_gather | solution.py:146
  131.8 16.9 gather_fusion.2
  240.3 295.2 %while.47 = (s32[]{:T(128)}, f32[12,128,64]{1,2,0:T(8,128)S(1)}, s32[]{:T(128)}, f32[8,256,12,64]{1,0,3,2:T(8,128)}, f32[8,12,128,64]{2,3,1,0:T(8,128)}, /*index...) while((s32[]{:T(128)}, f32[12,128,64]{1,2,0:T(8,128)S(1)}, ...), condition=%wide.region_8.9_spmd.clone, body=%wide.region_5.8_spmd.clone.sunk | while | flops 1313649664 | bytes 11765497 | solution.py:87
  254.1 18.5 dynamic_update_slice.85
  291.0 18.5 dynamic_update_slice.85
  327.9 18.5 dynamic_update_slice.85
  364.8 18.5 dynamic_update_slice.85
  401.7 18.5 dynamic_update_slice.85
  438.6 18.5 dynamic_update_slice.85
  475.5 18.5 dynamic_update_slice.85
  512.4 18.5 dynamic_update_slice.85
  625.6 466.3 %while.48 = (s32[]{:T(128)}, f32[12]{0:T(128)}, f32[12,128,64]{1,2,0:T(8,128)S(1)}, f32[8,256,12,64]{1,0,3,2:T(8,128)}, f32[8,256,128]{2,1,0:T(8,128)}, /*index=...) while((s32[]{:T(128)}, f32[12]{0:T(128)}, ...), condition=%wide.region_26.27_spmd.clone, body=%wide.region_13.26_spmd.clone.sunk | while | flops 3037355008 | bytes 28656244 | solution.py:87
  658.2 18.5 dynamic_update_slice.89
  716.5 18.5 dynamic_update_slice.89
  774.7 18.5 dynamic_update_slice.89
  832.9 18.5 dynamic_update_slice.89
  891.1 18.5 dynamic_update_slice.89
  949.3 18.5 dynamic_update_slice.89
  1007.5 18.5 dynamic_update_slice.89
  1065.7 18.5 dynamic_update_slice.89
  1107.1 16.9 multiply_reduce_fusion.13
  1181.7 593.2 %collective-permute-done = f32[2048,1536]{1,0:T(8,128)} collective-permute-done((f32[2048,1536]{1,0:T(8,128)}, f32[2048,1536]{1,0:T(8,128)}, u32[]{:S(2)}, u32[]{:S(2)}) %collective-permute-start) | collective-permute-done | bytes 12582944 | tf_op jit(solution)/shard_map/ppermute | solution.py:212
  1819.3 610.9 %all-reduce.30 = (bf16[2048,256]{1,0:T(8,128)(2,1)}, f32[4,256]{1,0:T(4,128)S(1)}, f32[256]{0:T(256)S(1)}) all-reduce(f32[2048,256]{1,0:T(8,128)S(1)} %fusion.112, f32[4,256]{1,0:T(4,128)S(1)} %pad_add_fusion.1, f32[256]{0:T(256)S(1)} %get-tuple-element.895), channel_id=1, replica_groups=mesh['dp'=8,'tensor'=4] {'tensor'}, use_global_device_ids=true, to_apply=%region_28.29 | all-reduce | flops 525568 | bytes 3155968 | tf_op jit(solution)/shard_map/psum | solution.py:235
  2444.2 25.3 all_to_all.45
  2469.5 24.1 all_to_all.46
  2512.4 25.1 all-reduce.24
  2540.7 42.4 %all-gather.12.cloned.1.call-done = bf16[2048,1536]{1,0:T(8,128)(2,1)} async-done(((bf16[2048,384]{1,0:T(8,128)(2,1)}), bf16[2048,1536]{1,0:T(8,128)(2,1)}) %all-gather.12.cloned.1.call-update) | async-done | bytes 6291472 | tf_op jit(solution)/shard_map/all_gather | solution.py:297
  2583.1 16.8 gather_fusion.3
  2599.9 98.3 %all-gather.10.cloned.1.call-done = bf16[2048,1536]{1,0:T(8,128)(2,1)} async-done(((bf16[2048,384]{1,0:T(8,128)(2,1)}), bf16[2048,1536]{1,0:T(8,128)(2,1)}) %all-gather.10.cloned.1.call-update) | async-done | bytes 6291472 | tf_op jit(solution)/shard_map/all_gather | solution.py:296
  2715.1 23.6 reduce-scatter.9.cloned.1.call-done
  2738.6 57.8 %reduce-scatter.11.cloned.1.call-done = f32[192,768]{1,0:T(8,128)} async-done(((f32[1536,768]{1,0:T(8,128)}), f32[192,768]{1,0:T(8,128)}) %reduce-scatter.11.cloned.1.call-update) | async-done | bytes 589840 | tf_op jit(solution)/shard_map/reduce_scatter | solution.py:265
  (1035 shorter events, 810.7 us)
Async XLA Ops:
  7.2 182.2 %all-gather.6.cloned.1.call-start = ((), (), s32[]{:S(2)}) async-start(), calls=%async_computation.8 | async-start | bytes 5308416 | tf_op jit(solution)/shard_map/all_gather | solution.py:144
  36.4 95.1 %copy-start.73 = (f32[12]{0:T(128)S(1)}, f32[12]{0:T(128)}, u32[]{:S(2)}) copy-start(f32[12]{0:T(128)} %param.34) | copy-start | bytes 148
  36.5 122.0 %all-to-all-start = ((bf16[8,256,1536]{2,1,0:T(8,128)(2,1)}), bf16[8,256,1536]{2,1,0:T(8,128)(2,1)}, u32[]{:S(2)}, u32[]{:S(2)}) async-start(bf16[8,256,1536]{2,1,0:T(8,128)(2,1)} %bitcast.440), calls=%async_computation | async-start | bytes 12582912 | tf_op jit(solution)/shard_map/all_to_all | solution.py:140
  41.6 528.3 %all-gather.8.cloned.1.call-start = ((), (), s32[]{:S(2)}) async-start(), calls=%async_computation.9 | async-start | bytes 2654208 | tf_op jit(solution)/shard_map/all_gather | solution.py:147
  131.6 46.9 %copy-start.16 = (bf16[1536,12]{0,1:T(8,128)(2,1)}, bf16[1536,12]{0,1:T(8,128)(2,1)S(1)}, u32[]{:S(2)}) copy-start(bf16[1536,12]{0,1:T(8,128)(2,1)S(1)} %reshape.579) | copy-start | bytes 110596
  131.6 46.9 %copy-start.61 = (f32[12]{0:T(128)}, f32[12]{0:T(128)S(1)}, u32[]{:S(2)}) copy-start(f32[12]{0:T(128)S(1)} %exp.96) | copy-start | bytes 148
  148.8 62.9 %copy-start.38 = (f32[768]{0:T(1024)}, f32[768]{0:T(1024)S(1)}, u32[]{:S(2)}) copy-start(f32[768]{0:T(1024)S(1)} %get-tuple-element.897) | copy-start | bytes 9220
  148.8 62.9 %copy-start.40 = (f32[768]{0:T(1024)}, f32[768]{0:T(1024)S(1)}, u32[]{:S(2)}) copy-start(f32[768]{0:T(1024)S(1)} %get-tuple-element.898) | copy-start | bytes 9220
  148.9 62.9 %copy-start.42 = (f32[768]{0:T(1024)}, f32[768]{0:T(1024)S(1)}, u32[]{:S(2)}) copy-start(f32[768]{0:T(1024)S(1)} %get-tuple-element.899) | copy-start | bytes 9220
  148.9 62.9 %copy-start.44 = (f32[768]{0:T(1024)}, f32[768]{0:T(1024)S(1)}, u32[]{:S(2)}) copy-start(f32[768]{0:T(1024)S(1)} %get-tuple-element.896) | copy-start | bytes 9220
  158.4 53.3 %copy-start.18 = (f32[2048]{0:T(1024)}, f32[2048]{0:T(1024)S(1)}, u32[]{:S(2)}) copy-start(f32[2048]{0:T(1024)S(1)} %get-tuple-element.1027) | copy-start | bytes 24580
  158.5 53.3 %copy-start.20 = (f32[2048]{0:T(1024)}, f32[2048]{0:T(1024)S(1)}, u32[]{:S(2)}) copy-start(f32[2048]{0:T(1024)S(1)} %get-tuple-element.1028) | copy-start | bytes 24580
  158.5 53.3 %copy-start.22 = (f32[2048]{0:T(1024)}, f32[2048]{0:T(1024)S(1)}, u32[]{:S(2)}) copy-start(f32[2048]{0:T(1024)S(1)} %get-tuple-element.1029) | copy-start | bytes 24580
  158.5 411.4 %all-to-all-start.2 = ((bf16[8,256,1536]{2,1,0:T(8,128)(2,1)}), bf16[8,256,1536]{2,1,0:T(8,128)(2,1)}, u32[]{:S(2)}, u32[]{:S(2)}) async-start(bf16[8,256,1536]{2,1,0:T(8,128)(2,1)} %bitcast.439), calls=%async_computation.2 | async-start | bytes 12582912 | tf_op jit(solution)/shard_map/all_to_all | solution.py:141
  163.3 2266.9 %all-reduce.29.cloned.1.call-start = ((), (), s32[]{:S(2)}) async-start(), calls=%async_computation.11 | async-start | bytes 25165824 | tf_op jit(solution)/shard_map/psum | solution.py:245
  710.1 32.1 %copy-start.37 = (s32[8,256]{1,0:T(8,128)S(1)}, s32[8,256]{1,0:T(8,128)}, u32[]{:S(2)}) copy-start(s32[8,256]{1,0:T(8,128)} %copy-done.36) | copy-start | bytes 24580 | tf_op jit(solution)/shard_map/transpose(jvp())/while
  768.4 32.1 %copy-start.37 = (s32[8,256]{1,0:T(8,128)S(1)}, s32[8,256]{1,0:T(8,128)}, u32[]{:S(2)}) copy-start(s32[8,256]{1,0:T(8,128)} %copy-done.36) | copy-start | bytes 24580 | tf_op jit(solution)/shard_map/transpose(jvp())/while
  826.6 32.1 %copy-start.37 = (s32[8,256]{1,0:T(8,128)S(1)}, s32[8,256]{1,0:T(8,128)}, u32[]{:S(2)}) copy-start(s32[8,256]{1,0:T(8,128)} %copy-done.36) | copy-start | bytes 24580 | tf_op jit(solution)/shard_map/transpose(jvp())/while
  1059.4 32.1 %copy-start.37 = (s32[8,256]{1,0:T(8,128)S(1)}, s32[8,256]{1,0:T(8,128)}, u32[]{:S(2)}) copy-start(s32[8,256]{1,0:T(8,128)} %copy-done.36) | copy-start | bytes 24580 | tf_op jit(solution)/shard_map/transpose(jvp())/while
  1149.8 1361.0 %reduce-scatter.13.cloned.1.call-start = ((), (), s32[]{:S(2)}) async-start(), calls=%async_computation.16 | async-start | bytes 884736
  1162.3 612.7 %collective-permute-start = (f32[2048,1536]{1,0:T(8,128)}, f32[2048,1536]{1,0:T(8,128)}, u32[]{:S(2)}, u32[]{:S(2)}) collective-permute-start(f32[2048,1536]{1,0:T(8,128)} %fusion.136), channel_id=1, source_target_pairs={{0,1},{1,0},{2,3},{3,2},{4,5},{5,4},{6,7},{7,6},{8,9},{9,8},{10,11... | collective-permute-start | bytes 37748744 | tf_op jit(solution)/shard_map/ppermute | solution.py:212
  1181.7 1355.8 %reduce-scatter.7.cloned.1.call-start = ((), (), s32[]{:S(2)}) async-start(), calls=%async_computation.13 | async-start | bytes 10616832 | tf_op jit(solution)/shard_map/reduce_scatter | solution.py:262
  1789.7 649.6 %collective-permute-start.1 = (f32[2048,1536]{1,0:T(8,128)}, f32[2048,1536]{1,0:T(8,128)}, u32[]{:S(2)}, u32[]{:S(2)}) collective-permute-start(f32[2048,1536]{1,0:T(8,128)} %add.264), channel_id=1, source_target_pairs={{0,2},{1,3},{2,0},{3,1},{4,6},{5,7},{6,4},{7,5},{8,10},{9,11},{10,... | collective-permute-start | bytes 37748744 | tf_op jit(solution)/shard_map/ppermute | solution.py:212
  1805.4 777.7 %all-gather.12.cloned.1.call-start = ((), (), s32[]{:S(2)}) async-start(), calls=%async_computation.12 | async-start | bytes 7864320 | tf_op jit(solution)/shard_map/all_gather | solution.py:297
  1818.6 611.7 %copy-start.12 = (bf16[1536,256]{1,0:T(8,128)(2,1)S(1)}, bf16[1536,256]{1,0:T(8,128)(2,1)}, u32[]{:S(2)}) copy-start(bf16[1536,256]{1,0:T(8,128)(2,1)} %copy-done.11) | copy-start | bytes 2359300
  1818.6 611.6 %copy-start.30 = (f32[2048]{0:T(1024)S(1)}, f32[2048]{0:T(1024)}, u32[]{:S(2)}) copy-start(f32[2048]{0:T(1024)} %copy-done.29) | copy-start | bytes 24580
  1818.6 611.6 %copy-start.32 = (f32[1536]{0:T(1024)S(1)}, f32[1536]{0:T(1024)}, u32[]{:S(2)}) copy-start(f32[1536]{0:T(1024)} %param.25) | copy-start | bytes 18436
  2444.2 49.5 %copy-start.13 = (bf16[2048,256]{1,0:T(8,128)(2,1)S(1)}, bf16[2048,256]{1,0:T(8,128)(2,1)}, u32[]{:S(2)}) copy-start(bf16[2048,256]{1,0:T(8,128)(2,1)} %get-tuple-element.971) | copy-start | bytes 3145732
  2469.5 228.7 %all-gather.10.cloned.1.call-start = ((), (), s32[]{:S(2)}) async-start(), calls=%async_computation.10 | async-start | bytes 7864320 | tf_op jit(solution)/shard_map/all_gather | solution.py:296
  2493.7 245.0 %reduce-scatter.9.cloned.1.call-start = ((), (), s32[]{:S(2)}) async-start(), calls=%async_computation.14 | async-start | bytes 1769472 | tf_op jit(solution)/shard_map/reduce_scatter | solution.py:263
  2499.7 296.8 %reduce-scatter.11.cloned.1.call-start = ((), (), s32[]{:S(2)}) async-start(), calls=%async_computation.15 | async-start | bytes 5308416 | tf_op jit(solution)/shard_map/reduce_scatter | solution.py:265
  2510.6 72.5 %copy-start.35 = (s32[2048]{0:T(1024)S(1)}, s32[2048]{0:T(1024)}, u32[]{:S(2)}) copy-start(s32[2048]{0:T(1024)} %get-tuple-element.985) | copy-start | bytes 24580
  (105 other events, 1102.1 us)
Sparse Core Ops, SparseCore 0:
  10.4 46.6 all-gather.5
  59.6 70.0 all-gather.7
  1149.9 719.2 all-reduce.28
  1872.8 38.8 reduce-scatter.12
  1915.0 76.6 reduce-scatter.6
  2469.6 113.4 all-gather.11
  2584.7 113.4 all-gather.9
  2702.1 36.5 reduce-scatter.8
  2742.7 53.7 reduce-scatter.10
